TPU v7x, 1024 devices: a whole 8x8x8 slice. The times are simulated.
1024 devices in a mesh: dp: 32 (over y_hi, z), ctx: 32 (over y_lo, x, core).
Axes of the slice: x: 8, y: 8 (y_hi: 4, y_lo: 2; y = y_hi * 2 + y_lo), z: 8, core: 2. Of those that a mesh axis runs over, the one named last changes fastest.
Arguments:
- emb: bfloat16 [32, 4096, 7168], P('dp', 'ctx'), may hold values from -6 to 6
- doc_lengths: int32 [32, 64], P('dp'), may hold values from 1 to 128, 4096 in all within a row
- latent: bfloat16 [32, 4096, 512], P('dp', 'ctx'), may hold values from -4 to 4
- q_latent: bfloat16 [32, 4096, 4, 512], P('dp', 'ctx'), may hold values from -32 to 32
- q_rope: bfloat16 [32, 4096, 256], P('dp', 'ctx'), may hold values from -12 to 12
- cotangent: bfloat16 [32, 4096, 4, 512], P('dp', 'ctx'), may hold values from -6 to 6
- gain: float32 [7168], replicated, may hold values from 0.1 to 1.9
- w_rope: bfloat16 [7168, 64], replicated, may hold values from -0.0625 to 0.0625
Outputs:
- grad_latent: bfloat16 [32, 4096, 512], P('dp', 'ctx')
- grad_rope_w: float32 [7168, 64], P(('dp', 'ctx'))
Inputs may be any that keep to these rules, and one draw needn't show every extreme that they name: `doc_lengths`: each sequence's lengths sum to 4096; some document has exactly 128 tokens.
All inputs are finite; a program needn't handle non-finite values.
Results may differ from a plain program's by a relative error of at most 0.014.
Values may be sent and summed in bfloat16 or wider, within the bound.
A program may use at most 32 MiB of HBM per device.

v0:
```python
import jax
import jax.numpy as jnp
from jax import lax
from jax.sharding import PartitionSpec as P

score_scale = 192.0 ** (-0.5)
norm_eps = 1e-06


def from_behind(block, axis, distance):
    devices = range(lax.axis_size(axis))
    route = [(i - distance, i) for i in devices if i - distance in devices]
    return lax.ppermute(block, axis, route)


def doc_lookup(doc_ends_src, places):
    doc_ends = jnp.cumsum(doc_ends_src)
    passed = doc_ends[None, :] <= places[:, None]
    doc_index = jnp.sum(passed.astype(jnp.int32), axis=1)
    doc_start = jnp.sum(jnp.where(passed, doc_ends_src[None, :], 0), axis=1)
    return (doc_index, doc_start)


def normed_rows(rows, keep_mask, gain):
    values = jnp.where(keep_mask[:, None], rows.astype(jnp.float32), 0.0)
    mean_sq = jnp.mean(values * values, axis=1, keepdims=True)
    return (values * lax.rsqrt(mean_sq + norm_eps) * gain[None, :]).astype(jnp.bfloat16)


def rotation(positions, half_width):
    frequency = 10000.0 ** (-jnp.arange(half_width).astype(jnp.float32) / half_width)
    angles = positions.astype(jnp.float32)[:, None] * frequency[None, :]
    return (jnp.cos(angles), jnp.sin(angles))


def rotate(raw_key, cosine, sine_table, half_width):
    leading, trailing = (raw_key[:, :half_width], raw_key[:, half_width:])
    return jnp.concatenate(
        [leading * cosine - trailing * sine_table, leading * sine_table + trailing * cosine], 1
    )


def unrotate(key_grad, cosine, sine_table, half_width):
    leading, trailing = (key_grad[:, :half_width], key_grad[:, half_width:])
    return jnp.concatenate(
        [leading * cosine + trailing * sine_table, trailing * cosine - leading * sine_table], 1
    )


def contract_rows(left, right):
    return lax.dot_general(
        left, right, (((0,), (0,)), ((), ())), preferred_element_type=jnp.float32
    )


def contract_cols(left, right):
    return lax.dot_general(
        left, right, (((1,), (1,)), ((), ())), preferred_element_type=jnp.float32
    )


def weight_product(normed, raw_grad):
    return lax.dot_general(
        normed.astype(jnp.float32),
        raw_grad,
        (((0,), (0,)), ((), ())),
        precision=lax.Precision.HIGHEST,
        preferred_element_type=jnp.float32,
    )


def key_gradients(query_lat, query_rope, cot_rows, keys_lat, keys_rope, allowed):
    scores = (
        contract_cols(query_lat, keys_lat) + contract_cols(query_rope, keys_rope)
    ) * score_scale
    scores = jnp.where(allowed, scores, -1e30)
    highest = jnp.max(scores, axis=1, keepdims=True)
    exponent = jnp.where(allowed, jnp.exp(scores - highest), 0.0)
    probs = exponent / jnp.sum(exponent, axis=1, keepdims=True)
    weights = probs.astype(jnp.bfloat16)
    dprobs = contract_cols(cot_rows, keys_lat)
    centre = jnp.sum(probs * dprobs, axis=1, keepdims=True)
    score_grad = (score_scale * probs * (dprobs - centre)).astype(jnp.bfloat16)
    lat_grad = contract_rows(weights, cot_rows) + contract_rows(score_grad, query_lat)
    rope_grad = contract_rows(score_grad, query_rope)
    return (lat_grad, rope_grad)


def per_device(emb, doc_lengths, latent, q_latent, q_rope, cotangent, gain, w_rope):
    tokens_here = emb.shape[1]
    head_count = q_latent.shape[2]
    lat_width = latent.shape[2]
    rope_width = w_rope.shape[1]
    half_width = rope_width // 2
    ctx_count = lax.axis_size("ctx")
    data_count = lax.axis_size("dp")
    seq_length = tokens_here * ctx_count
    offset = lax.axis_index("ctx") * tokens_here
    lengths_row = doc_lengths[0]
    places = offset + jnp.arange(tokens_here, dtype=jnp.int32)
    doc_index, doc_start = doc_lookup(lengths_row, places)
    next_index, unused_start = doc_lookup(lengths_row, places + 1)
    incoming = from_behind(emb[0, :1, :], "ctx", -1)
    shifted = jnp.concatenate([emb[0, 1:, :], incoming], 0)
    keep_mask = (next_index == doc_index) & (places + 1 < seq_length)
    normed = normed_rows(shifted, keep_mask, gain)
    raw_key = jnp.dot(normed, w_rope, preferred_element_type=jnp.float32)
    cosine, sine_table = rotation(places - doc_start, half_width)
    key_rope = rotate(raw_key, cosine, sine_table, half_width).astype(jnp.bfloat16)
    own_lat = latent[0]
    prev_lat, prev_rope = from_behind((own_lat, key_rope), "ctx", 1)
    k_places = offset - tokens_here + jnp.arange(2 * tokens_here, dtype=jnp.int32)
    k_doc, unused_kstart = doc_lookup(lengths_row, k_places)
    allowed = (
        (k_places[None, :] >= 0)
        & (k_places[None, :] <= places[:, None])
        & (k_doc[None, :] == doc_index[:, None])
    )
    allowed = jnp.repeat(allowed, head_count, axis=0)
    query_lat = q_latent[0].reshape(tokens_here * head_count, lat_width)
    query_rope = q_rope[0].reshape(tokens_here * head_count, rope_width)
    cot_rows = cotangent[0].reshape(tokens_here * head_count, lat_width)
    keys_lat = jnp.concatenate([prev_lat, own_lat], 0)
    keys_rope = jnp.concatenate([prev_rope, key_rope], 0)
    lat_grad, rope_grad = key_gradients(
        query_lat, query_rope, cot_rows, keys_lat, keys_rope, allowed
    )
    back_lat, back_rope = from_behind((lat_grad[:tokens_here], rope_grad[:tokens_here]), "ctx", -1)
    lat_total = lat_grad[tokens_here:] + back_lat
    rope_total = rope_grad[tokens_here:] + back_rope
    grad_latent = lat_total.astype(jnp.bfloat16)[None]
    key_grad_raw = unrotate(rope_total, cosine, sine_table, half_width)
    weight_part = weight_product(normed, key_grad_raw)
    loss_scale = float(data_count * seq_length) ** (-0.5)
    reduced = lax.psum_scatter(weight_part, "dp", scatter_dimension=0, tiled=True)
    reduced = lax.psum_scatter(reduced, "ctx", scatter_dimension=0, tiled=True)
    return (grad_latent, reduced * loss_scale)


def solution(mesh):
    placed = (
        P("dp", "ctx", None),
        P("dp", None),
        P("dp", "ctx", None),
        P("dp", "ctx", None, None),
        P("dp", "ctx", None),
        P("dp", "ctx", None, None),
        P(),
        P(),
    )
    return jax.shard_map(
        per_device,
        mesh=mesh,
        in_specs=placed,
        out_specs=(P("dp", "ctx", None), P(("dp", "ctx"), None)),
        check_vma=False,
    )
```

profile of v0, /device:TPU:1, one launch (start us, length us, event | category | flops | bytes accessed | tf_op | source)
XLA Modules:
  0.0 403.2 jit_solution(8209364268949967218)
XLA Ops:
  7.2 0.0 copy-start
  7.2 0.0 reduce-scatter.5.cloned.1.call-start
  7.2 1.0 slice_bitcast_fusion.1
  8.2 16.0 %collective-permute-start.1 = (bf16[1,7168]{1,0:T(2,128)(2,1)S(1)}, bf16[1,7168]{1,0:T(2,128)(2,1)S(1)}, u32[]{:S(2)}, u32[]{:S(2)}) collective-permute-start(bf16[1,7168]{1,0:T(2,128)(2,1)S(1)} %slice_bitcast_fusion.1), channel_id=1, source_target_pairs={{1,0},{2,1},{3,2},{4,3},{5,4},{6,5},{7,6},{8,7},{9,8},{10,9},{11,1... | collective-permute-start | bytes 43016 | tf_op jit(solution)/shard_map/ppermute | solution.py:13
  24.3 1.9 collective-permute-start
  26.2 1.9 slice_bitcast_fusion
  28.2 0.1 copy.20
  28.3 0.1 reduce-window.8
  28.4 0.1 reduce
  28.5 0.1 convert_reduce_fusion
  28.6 0.1 fusion.10
  28.8 0.7 multiply_reduce_fusion
  29.5 0.9 fusion.40
  30.5 0.1 fusion.30
  30.6 0.6 pad_maximum_fusion.4
  31.2 1.9 collective-permute-start.2
  33.1 0.1 compare_and_fusion
  33.3 0.9 reshape_squeeze.11
  34.2 0.1 broadcast_in_dim.37
  34.3 0.1 reshape.88
  34.5 0.2 copy.22
  34.7 1.0 reshape_squeeze.10
  35.7 1.2 reshape_squeeze.9
  36.9 1.0 fusion.11
  38.0 1.3 fusion.41
  39.3 0.1 fusion.4
  39.5 1.6 multiply_reduce_fusion.1
  41.1 1.1 multiply_convert_fusion.1
  42.2 1.1 fusion.42
  43.3 3.0 collective-permute-start.4
  46.3 2.2 collective-permute-done.4
  48.6 0.1 fusion.33
  48.8 4.2 %fusion.17 = f32[7168,64]{1,0:T(8,128)} fusion(f32[128,32]{0,1:T(8,128)S(1)} %get-tuple-element.14, f32[128,32]{0,1:T(8,128)S(1)} %get-tuple-element.13, f32[7168]{0:T(1024)S(1)} %copy-done.18, f32[128]{0:T(128)S(1)} %copy-done.20, pred[128]{0:T(512)(128)(4,1)S(1)} %copy-done.16, bf16[1,7168]{1,0:T(2,128)(2,1)S(1)} %copy-done.9, ...), kind=kOutput, calls=%fused_computation.35 | convolution fusion | flops 711991296 | bytes 3732096
  52.9 0.0 reduce-scatter.5.cloned.1.call-update
  52.9 1.0 copy-done.2
  54.0 0.0 copy-done.4
  54.0 0.2 copy-done.7
  54.2 0.3 fusion.6
  54.5 0.3 convolution_add_fusion
  54.8 1.9 collective-permute-start.3
  56.7 1.3 dynamic-slice
  58.7 3.8 collective-permute-done.3
  62.5 0.7 fusion.8
  63.2 226.3 %reduce-scatter.5.cloned.1.call-done = f32[224,64]{1,0:T(8,128)} async-done(((f32[7168,64]{1,0:T(8,128)}), f32[224,64]{1,0:T(8,128)}) %reduce-scatter.5.cloned.1.call-update) | async-done | bytes 57360
  289.5 1.0 copy.25
  290.4 105.1 %all-reduce = f32[224,64]{0,1:T(8,128)S(1)} all-reduce(f32[224,64]{0,1:T(8,128)S(1)} %copy.25), channel_id=3, replica_groups=mesh['dp'=32,'ctx'=32] {'ctx'}, use_global_device_ids=true, to_apply=%region_10.11.clone | all-reduce | flops 14336 | bytes 114688
  395.6 0.1 dynamic-slice_multiply_fusion
  395.6 0.7 copy.23
  (51 shorter events, 0.2 us)
Async XLA Ops:
  7.2 22.3 %copy-start = (bf16[7168,64]{0,1:T(8,128)(2,1)S(1)}, bf16[7168,64]{0,1:T(8,128)(2,1)}, u32[]{:S(2)}) copy-start(bf16[7168,64]{0,1:T(8,128)(2,1)} %param.15) | copy-start | bytes 2752516
  7.2 21.0 %copy-start.14 = (s32[1,64]{1,0:T(1,128)S(1)}, s32[1,64]{1,0:T(1,128)}, u32[]{:S(2)}) copy-start(s32[1,64]{1,0:T(1,128)} %param.9) | copy-start | bytes 772
  7.2 22.3 %copy-start.17 = (f32[7168]{0:T(1024)S(1)}, f32[7168]{0:T(1024)}, u32[]{:S(2)}) copy-start(f32[7168]{0:T(1024)} %param.14) | copy-start | bytes 86020
  7.2 282.3 %reduce-scatter.5.cloned.1.call-start = ((), (), s32[]{:S(2)}) async-start(), calls=%async_computation.1 | async-start | bytes 3784704
  8.2 20.5 %collective-permute-start.1 = (bf16[1,7168]{1,0:T(2,128)(2,1)S(1)}, bf16[1,7168]{1,0:T(2,128)(2,1)S(1)}, u32[]{:S(2)}, u32[]{:S(2)}) collective-permute-start(bf16[1,7168]{1,0:T(2,128)(2,1)S(1)} %slice_bitcast_fusion.1), channel_id=1, source_target_pairs={{1,0},{2,1},{3,2},{4,3},{5,4},{6,5},{7,6},{8,7},{9,8},{10,9},{11,1... | collective-permute-start | bytes 43016 | tf_op jit(solution)/shard_map/ppermute | solution.py:13
  24.3 13.7 %collective-permute-start = (bf16[128,512]{1,0:T(8,128)(2,1)}, bf16[128,512]{1,0:T(8,128)(2,1)}, u32[]{:S(2)}, u32[]{:S(2)}) collective-permute-start(bf16[128,512]{1,0:T(8,128)(2,1)} %bitcast.28), channel_id=1, source_target_pairs={{0,1},{1,2},{2,3},{3,4},{4,5},{5,6},{6,7},{7,8},{8,9},{9,10},{10,1... | collective-permute-start | bytes 393224 | tf_op jit(solution)/shard_map/ppermute | solution.py:13
  28.7 1.7 copy-start.10
  28.7 1.7 copy-start.15
  28.8 1.7 copy-start.12
  28.8 1.7 copy-start.8
  29.5 1.0 copy-start.19
  29.5 3.7 copy-start.6
  31.2 5.7 %collective-permute-start.2 = (bf16[128,64]{0,1:T(8,128)(2,1)}, bf16[128,64]{0,1:T(8,128)(2,1)}, u32[]{:S(2)}, u32[]{:S(2)}) collective-permute-start(bf16[128,64]{0,1:T(8,128)(2,1)} %pad_maximum_fusion.4), channel_id=1, source_target_pairs={{0,1},{1,2},{2,3},{3,4},{4,5},{5,6},{6,7},{7,8},{8,9},{9,10},{10,1... | collective-permute-start | bytes 49160 | tf_op jit(solution)/shard_map/ppermute | solution.py:13
  34.7 6.4 %copy-start.3 = (pred[512,256]{0,1:T(32,128)(4,1)}, pred[512,256]{0,1:T(32,128)(4,1)S(1)}, u32[]{:S(2)}) copy-start(pred[512,256]{0,1:T(32,128)(4,1)S(1)} %copy.22) | copy-start | bytes 393220
  35.7 5.4 %copy-start.5 = (bf16[512,64]{1,0:T(8,128)(2,1)}, bf16[512,64]{1,0:T(8,128)(2,1)S(1)}, u32[]{:S(2)}) copy-start(bf16[512,64]{1,0:T(8,128)(2,1)S(1)} %reshape_squeeze.10) | copy-start | bytes 196612
  37.9 10.6 %copy-start.11 = (f32[128]{0:T(128)S(1)}, f32[128]{0:T(128)}, u32[]{:S(2)}) copy-start(f32[128]{0:T(128)} %copy-done.10) | copy-start | bytes 1540
  37.9 10.6 %copy-start.13 = (f32[32]{0:T(128)S(1)}, f32[32]{0:T(128)}, u32[]{:S(2)}) copy-start(f32[32]{0:T(128)} %copy-done.12) | copy-start | bytes 388
  37.9 10.8 %copy-start.9 = (bf16[1,7168]{1,0:T(2,128)(2,1)S(1)}, bf16[1,7168]{1,0:T(2,128)(2,1)}, u32[]{:S(2)}) copy-start(bf16[1,7168]{1,0:T(2,128)(2,1)} %copy-done.8) | copy-start | bytes 43012
  37.9 10.8 %copy-start.16 = (pred[128]{0:T(512)(128)(4,1)S(1)}, pred[128]{0:T(512)(128)(4,1)}, u32[]{:S(2)}) copy-start(pred[128]{0:T(512)(128)(4,1)} %copy-done.15) | copy-start | bytes 388
  37.9 10.8 %copy-start.18 = (f32[7168]{0:T(1024)S(1)}, f32[7168]{0:T(1024)}, u32[]{:S(2)}) copy-start(f32[7168]{0:T(1024)} %param.14) | copy-start | bytes 86020
  38.0 10.8 %copy-start.20 = (f32[128]{0:T(128)S(1)}, f32[128]{0:T(128)}, u32[]{:S(2)}) copy-start(f32[128]{0:T(128)} %copy-done.19) | copy-start | bytes 1540
  39.3 1.8 copy-start.1
  43.3 5.2 %collective-permute-start.4 = (f32[128,64]{0,1:T(8,128)S(1)}, f32[128,64]{0,1:T(8,128)S(1)}, u32[]{:S(2)}, u32[]{:S(2)}) collective-permute-start(f32[128,64]{0,1:T(8,128)S(1)} %slice.45), channel_id=1, source_target_pairs={{1,0},{2,1},{3,2},{4,3},{5,4},{6,5},{7,6},{8,7},{9,8},{10,9},{11,1... | collective-permute-start | bytes 98312 | tf_op jit(solution)/shard_map/ppermute | solution.py:13
  52.9 1.0 copy-start.2
  52.9 1.1 copy-start.4
  52.9 1.2 copy-start.7
  54.8 7.7 %collective-permute-start.3 = (f32[128,512]{1,0:T(8,128)S(1)}, f32[128,512]{1,0:T(8,128)S(1)}, u32[]{:S(2)}, u32[]{:S(2)}) collective-permute-start(f32[128,512]{1,0:T(8,128)S(1)} %slice.43), channel_id=1, source_target_pairs={{1,0},{2,1},{3,2},{4,3},{5,4},{6,5},{7,6},{8,7},{9,8},{10,9},{11,1... | collective-permute-start | bytes 786440 | tf_op jit(solution)/shard_map/ppermute | solution.py:13
Sparse Core Ops, SparseCore 0:
  53.1 236.3 reduce-scatter.4
where the time goes:
time: 406 us; the launch traced here: 403 us
  waiting for transfers between devices  232 us (57%)
  blocking collectives  105 us (26%)
  starting transfers between devices  24.8 us (6%)
  between operations  15.2 us (4%)
  local copies, waits for them, and re-layouts  10.9 us (3%)
  matrix products  10.6 us (3%)
  other arithmetic  4.16 us (1%)
    unnamed x2, waiting for transfers between devices  226 us
    unnamed x1, blocking collectives  105 us
    ppermute x5, starting transfers between devices, from_behind(): return lax.ppermute(block, axis, route)  24.8 us
  transfers between devices with their start and end apart: 6, of which 3 were waited for; matrix products, arithmetic and copies ran while one was open for 3% of the time, Pallas kernels for 0%

commit v1 on v0

--- a/solution.py
+++ b/solution.py
@@ -1,7 +1,235 @@
 import jax
 import jax.numpy as jnp
 from jax import lax
+from jax.experimental import pallas as pl
+from jax.experimental.pallas import tpu as pltpu
 from jax.sharding import PartitionSpec as P
+
+MESH = pl.DeviceIdType.MESH
+F32 = jnp.float32
+BF16 = jnp.bfloat16
+UNITS = (3, 2, 2)
+FIRST_UNIT = (0, 3, 5)
+ROW_START = (0, 768, 1280)
+ORDER = (4, 3, 5, 2, 6, 1, 7)
+
+
+def place():
+    d, c = lax.axis_index("dp"), lax.axis_index("ctx")
+    return {
+        "core": c % 2,
+        "x": (c // 2) % 8,
+        "y": (d // 8) * 2 + c // 16,
+        "z": d % 8,
+    }
+
+
+def device(at, **moved):
+    p = {**at, **moved}
+    return ((p["y"] // 2) * 8 + p["z"], ((p["y"] % 2) * 8 + p["x"]) * 2 + p["core"])
+
+
+STAGES = (("x", "z", "y"), ("y", "x", "z"), ("z", "x", "y"))
+
+
+def step_of(axis, i):
+    if axis == "x":
+        return i * 14
+    if axis == "z":
+        return i * 224
+    return (i // 2) * 1792 + (i % 2) * 112
+
+
+def transpose_rows(e_ref, et_ref):
+    def body(i, carry):
+        for k in range(8):
+            at = pl.multiple_of(i * 1024 + k * 128, 128)
+            et_ref[pl.ds(at, 128), :] = e_ref[:, pl.ds(at, 128)].astype(F32).T
+        return carry
+
+    lax.fori_loop(0, 7, body, 0)
+
+
+def build_left(et_ref, left_ref):
+    def body(a, carry):
+        for color, (first, second, third) in enumerate(STAGES):
+            units = UNITS[color]
+            stride = step_of(second, 1)
+            for unit in range(units):
+                for q in range(2):
+                    for half in range(2):
+                        for pair in range(2):
+                            rows = []
+                            for p in (2 * pair, 2 * pair + 1):
+                                base = (
+                                    step_of(first, a)
+                                    + step_of(third, 2 * p + half)
+                                    + q * 7
+                                    + FIRST_UNIT[color]
+                                    + unit
+                                )
+                                rows.append(et_ref[pl.ds(base, 8, stride=stride), :])
+                            at = ROW_START[color] + a * (units * 32) + unit * 32 + pair * 16
+                            left_ref[
+                                q, pl.ds(pl.multiple_of(at, 16), 16), half * 128 : half * 128 + 128
+                            ] = jnp.concatenate(rows, 0).astype(BF16)
+        return carry
+
+    lax.fori_loop(0, 8, body, 0)
+
+
+def rs_scratch():
+    shapes = [
+        pltpu.VMEM((7168, 128), F32),
+        pltpu.VMEM((2, 1792, 256), BF16),
+        pltpu.VMEM((1792, 128), BF16),
+        pltpu.VMEM((1792, 128), BF16),
+        pltpu.VMEM((1792, 128), F32),
+        pltpu.SemaphoreType.DMA((3,)),
+        pltpu.SemaphoreType.DMA((3,)),
+        pltpu.SemaphoreType.DMA((3, 3, 8)),
+        pltpu.SemaphoreType.DMA((3, 3, 8)),
+    ]
+    for n in UNITS:
+        shapes += [
+            pltpu.VMEM((8, n * 32, 128), BF16),
+            pltpu.VMEM((8, n * 32, 128), BF16),
+            pltpu.VMEM((n * 32, 128), F32),
+            pltpu.VMEM((8, n * 4, 128), F32),
+            pltpu.VMEM((8, n * 4, 128), F32),
+            pltpu.VMEM((n * 4, 128), F32),
+            pltpu.VMEM((4, n, 128), F32),
+            pltpu.VMEM((8, n, 128), F32),
+        ]
+    return shapes
+
+
+def greet(at, barrier):
+    for axis in ("x", "y", "z"):
+        for step in range(1, 8):
+            pl.semaphore_signal(
+                barrier,
+                inc=1,
+                device_id=device(at, **{axis: (at[axis] + step) % 8}),
+                device_id_type=MESH,
+            )
+    pl.semaphore_signal(barrier, inc=1, device_id=device(at, core=1 - at["core"]), device_id_type=MESH)
+
+
+GREETED = 22
+
+
+def reduce_scatter(at, right, out_ref, scale, left_ref, c_send, c_recv, own, c_ss, c_rs, ss, rs, bufs):
+    core = at["core"]
+    partner = device(at, core=1 - core)
+    pending = []
+    core_copies = []
+    for color, n in enumerate(UNITS):
+        rows = pl.ds(ROW_START[color], n * 256)
+        c_send[rows, :] = jnp.dot(
+            left_ref[1 - core, rows, :], right, preferred_element_type=F32
+        ).astype(BF16)
+        copy = pltpu.make_async_remote_copy(
+            src_ref=c_send.at[rows],
+            dst_ref=c_recv.at[rows],
+            send_sem=c_ss.at[color],
+            recv_sem=c_rs.at[color],
+            device_id=partner,
+            device_id_type=MESH,
+        )
+        copy.start()
+        core_copies.append(copy)
+    own[...] = jnp.dot(left_ref[core], right, preferred_element_type=F32)
+
+    def send(color, stage, source_of, target):
+        axis = STAGES[color][stage]
+        for step in ORDER:
+            to = (at[axis] + step) % 8
+            copy = pltpu.make_async_remote_copy(
+                src_ref=source_of(to),
+                dst_ref=target.at[step],
+                send_sem=ss.at[color, stage, step],
+                recv_sem=rs.at[color, stage, step],
+                device_id=device(at, **{axis: to}),
+                device_id_type=MESH,
+            )
+            copy.start()
+            pending.append((color, stage, copy))
+
+    def arrived(color, stage):
+        for c, s, copy in pending:
+            if (c, s) == (color, stage):
+                copy.wait_recv()
+
+    def total(first, target):
+        value = first.astype(F32)
+        for step in range(1, 8):
+            value = value + target[step].astype(F32)
+        return value
+
+    for color, n in enumerate(UNITS):
+        s1, r1, t1, s2, r2, t2, s3, r3 = bufs[color]
+        core_copies[color].wait_recv()
+        for a in range(8):
+            rows = pl.ds(ROW_START[color] + a * n * 32, n * 32)
+            s1[a] = (own[rows, :] + c_recv[rows, :].astype(F32)).astype(BF16)
+        send(color, 0, lambda to: s1.at[to], r1)
+    for color, n in enumerate(UNITS):
+        s1, r1, t1, s2, r2, t2, s3, r3 = bufs[color]
+        arrived(color, 0)
+        t1[...] = total(s1[at[STAGES[color][0]]], r1)
+        for b in range(8):
+            s2[b] = t1[pl.ds(b, n * 4, stride=8), :]
+        send(color, 1, lambda to: s2.at[to], r2)
+    for color, n in enumerate(UNITS):
+        s1, r1, t1, s2, r2, t2, s3, r3 = bufs[color]
+        arrived(color, 1)
+        t2[...] = total(s2[at[STAGES[color][1]]], r2)
+        for p in range(4):
+            s3[p] = t2[pl.ds(p, n, stride=4), :]
+        send(color, 2, lambda to: s3.at[to // 2], r3)
+    for color, n in enumerate(UNITS):
+        s1, r1, t1, s2, r2, t2, s3, r3 = bufs[color]
+        arrived(color, 2)
+        last = at[STAGES[color][2]]
+        value = total(s3[last // 2], r3) * scale
+        value = jnp.where(last % 2 == 0, value, pltpu.roll(value, 64, 1))
+        out_ref[FIRST_UNIT[color] : FIRST_UNIT[color] + n, :] = value[:, :64]
+    for copy in core_copies:
+        copy.wait_send()
+    for _, _, copy in pending:
+        copy.wait_send()
+
+
+def rs_kernel(scale, e_ref, g_ref, out_ref, et, left, c_send, c_recv, own, c_ss, c_rs, ss, rs, *bufs):
+    at = place()
+    barrier = pltpu.get_barrier_semaphore()
+    greet(at, barrier)
+    transpose_rows(e_ref, et)
+    build_left(et, left)
+    g = g_ref[...]
+    lane = lax.broadcasted_iota(jnp.int32, g.shape, 1)
+    right = jnp.concatenate(
+        [jnp.where(lane < 64, g, 0.0), jnp.where(lane < 64, 0.0, g)], 0
+    ).astype(BF16)
+    pl.semaphore_wait(barrier, GREETED)
+    bufs = [bufs[8 * i : 8 * i + 8] for i in range(3)]
+    reduce_scatter(at, right, out_ref, scale, left, c_send, c_recv, own, c_ss, c_rs, ss, rs, bufs)
+
+
+def weight_gradient(normed, raw_grad, scale):
+    return pl.pallas_call(
+        lambda *refs: rs_kernel(scale, *refs),
+        out_shape=jax.ShapeDtypeStruct((7, 64), F32),
+        in_specs=[pl.BlockSpec(memory_space=pltpu.VMEM)] * 2,
+        out_specs=pl.BlockSpec(memory_space=pltpu.VMEM),
+        scratch_shapes=rs_scratch(),
+        compiler_params=pltpu.CompilerParams(
+            collective_id=0, has_side_effects=True, vmem_limit_bytes=60 * 1024 * 1024
+        ),
+        name="weight_gradient",
+    )(normed, jnp.concatenate([raw_grad, raw_grad], 1))
+
 
 score_scale = 192.0 ** (-0.5)
 norm_eps = 1e-06
@@ -56,16 +284,6 @@
 def contract_cols(left, right):
     return lax.dot_general(
         left, right, (((1,), (1,)), ((), ())), preferred_element_type=jnp.float32
-    )
-
-
-def weight_product(normed, raw_grad):
-    return lax.dot_general(
-        normed.astype(jnp.float32),
-        raw_grad,
-        (((0,), (0,)), ((), ())),
-        precision=lax.Precision.HIGHEST,
-        preferred_element_type=jnp.float32,
     )
 
 
@@ -130,11 +348,9 @@
     rope_total = rope_grad[tokens_here:] + back_rope
     grad_latent = lat_total.astype(jnp.bfloat16)[None]
     key_grad_raw = unrotate(rope_total, cosine, sine_table, half_width)
-    weight_part = weight_product(normed, key_grad_raw)
     loss_scale = float(data_count * seq_length) ** (-0.5)
-    reduced = lax.psum_scatter(weight_part, "dp", scatter_dimension=0, tiled=True)
-    reduced = lax.psum_scatter(reduced, "ctx", scatter_dimension=0, tiled=True)
-    return (grad_latent, reduced * loss_scale)
+    grad_rope_w = weight_gradient(normed, key_grad_raw, loss_scale)
+    return (grad_latent, grad_rope_w)
 
 
 def solution(mesh):

time: 406 us -> 72.6 us (0.18)
  waiting for transfers between devices: 232 us -> 1.64 us
  blocking collectives: 105 us -> 0 us
  Pallas kernels: 0 us -> 31.5 us
  between operations: 15.2 us -> 0.99 us
  matrix products: 10.6 us -> 2.42 us
  local copies, waits for them, and re-layouts: 10.9 us -> 6.44 us
    unnamed x2 -> x0, waiting for transfers between devices: 226 us -> none
    unnamed x1 -> x0, blocking collectives: 105 us -> none
    pallas_call x0 -> x1, Pallas kernels: none -> 31.5 us  [weight_gradient(): pl.pallas_call(lambda *refs: rs_kernel(scale, *refs), out_shape=jax.Shape...]
    ppermute x5, waiting for transfers between devices: 6.08 us -> 1.64 us  [from_behind(): return lax.ppermute(block, axis, route)]
    unnamed x1 -> x0, matrix products: 4.16 us -> none
  transfers between devices with their start and end apart: 6 -> 5, of which waited for: 3 -> 2; matrix products, arithmetic and copies ran while one was open for 3% -> 10% of each run, Pallas kernels for 0% -> 44%
where the time goes in v1:
time: 72.6 us; the launch traced here: 71.5 us
  Pallas kernels  31.5 us (43%)
  starting transfers between devices  24 us (33%)
  local copies, waits for them, and re-layouts  6.44 us (9%)
  other arithmetic  4.45 us (6%)
  matrix products  2.42 us (3%)
  waiting for transfers between devices  1.64 us (2%)
  between operations  0.99 us (1%)
    pallas_call x1, Pallas kernels, weight_gradient(): pl.pallas_call(lambda *refs: rs_kernel(scale, *refs), out_shape=jax.Shape...  31.5 us
    ppermute x5, starting transfers between devices, from_behind(): return lax.ppermute(block, axis, route)  24 us
    unnamed x17, local copies, waits for them, and re-layouts  2.56 us
    squeeze x1, local copies, waits for them, and re-layouts, per_device(): shifted = jnp.concatenate([emb[0, 1:, :], incoming], 0)  1.95 us
    ppermute x5, waiting for transfers between devices, from_behind(): return lax.ppermute(block, axis, route)  1.64 us
  transfers between devices with their start and end apart: 5, of which 2 were waited for; matrix products, arithmetic and copies ran while one was open for 10% of the time, Pallas kernels for 44%

profile of v1, /device:TPU:1, one launch (start us, length us, event | category | flops | bytes accessed | tf_op | source)
XLA Modules:
  0.0 71.5 jit_solution(13407793681549063786)
XLA Ops:
  0.6 0.0 copy-start
  0.6 1.0 %slice_bitcast_fusion.1 = bf16[1,7168]{1,0:T(2,128)(2,1)S(1)} fusion(bf16[1,128,7168]{2,1,0:T(8,128)(2,1)} %param.8), kind=kLoop, calls=%fused_computation.54 | loop fusion | bytes 28672 | tf_op jit(solution)/shard_map/squeeze | solution.py:321
  1.6 16.0 %collective-permute-start.1 = (bf16[1,7168]{1,0:T(2,128)(2,1)S(1)}, bf16[1,7168]{1,0:T(2,128)(2,1)S(1)}, u32[]{:S(2)}, u32[]{:S(2)}) collective-permute-start(bf16[1,7168]{1,0:T(2,128)(2,1)S(1)} %slice_bitcast_fusion.1), channel_id=1, source_target_pairs={{1,0},{2,1},{3,2},{4,3},{5,4},{6,5},{7,6},{8,7},{9,8},{10,9},{11,1... | collective-permute-start | bytes 43016 | tf_op jit(solution)/shard_map/ppermute | solution.py:241
  17.7 1.9 %collective-permute-start = (bf16[128,512]{1,0:T(8,128)(2,1)}, bf16[128,512]{1,0:T(8,128)(2,1)S(1)}, u32[]{:S(2)}, u32[]{:S(2)}) collective-permute-start(bf16[128,512]{1,0:T(8,128)(2,1)} %bitcast.25), channel_id=1, source_target_pairs={{0,1},{1,2},{2,3},{3,4},{4,5},{5,6},{6,7},{7,8},{8,9},{9,10},{10,1... | collective-permute-start | bytes 393224 | tf_op jit(solution)/shard_map/ppermute | solution.py:241
  19.6 0.0 copy-start.7
  19.6 1.9 %slice_bitcast_fusion = bf16[127,7168]{1,0:T(8,128)(2,1)S(1)} fusion(bf16[1,128,7168]{2,1,0:T(8,128)(2,1)} %param.8), kind=kLoop, calls=%fused_computation.4 | loop fusion | bytes 3641344 | tf_op jit(solution)/shard_map/squeeze | solution.py:322
  21.6 0.0 copy-start.6
  21.6 0.1 copy.29
  21.7 0.1 reduce-window.8
  21.8 0.1 reduce
  21.9 0.1 fusion.30
  22.1 0.1 convert_reduce_fusion
  22.2 0.0 collective-permute-done.1
  22.2 0.7 multiply_reduce_fusion
  22.9 0.7 multiply_convert_fusion.refs_0_
  23.6 1.2 %copy-done.1 = bf16[128,7168]{1,0:T(8,128)(2,1)} copy-done((bf16[128,7168]{1,0:T(8,128)(2,1)}, bf16[128,7168]{1,0:T(8,128)(2,1)S(1)}, u32[]{:S(2)}) %copy-start.1) | copy-done | bytes 1835032
  24.8 0.6 fusion.36
  25.5 0.0 copy-start.3
  25.5 0.3 fusion.18
  25.8 0.1 pad_maximum_fusion.5
  25.9 1.9 %collective-permute-start.2 = (bf16[128,64]{1,0:T(8,128)(2,1)S(1)}, bf16[128,64]{1,0:T(8,128)(2,1)S(1)}, u32[]{:S(2)}, u32[]{:S(2)}) collective-permute-start(bf16[128,64]{1,0:T(8,128)(2,1)S(1)} %pad_maximum_fusion.5), channel_id=1, source_target_pairs={{0,1},{1,2},{2,3},{3,4},{4,5},{5,6},{6,7},{7,8},{8,9},{9,10},{10,1... | collective-permute-start | bytes 49160 | tf_op jit(solution)/shard_map/ppermute | solution.py:241
  27.8 0.1 compare_and_fusion
  28.0 0.0 copy-start.4
  28.0 0.1 reshape_squeeze.10
  28.1 0.1 broadcast_in_dim.37
  28.2 0.1 reshape.88
  28.4 0.2 copy.34
  28.6 0.1 reshape_squeeze.9
  28.7 0.1 reshape_squeeze.11
  28.9 0.2 collective-permute-done.2
  29.0 0.2 fusion.23
  29.2 0.0 collective-permute-done
  29.3 0.4 fusion.35
  29.6 0.1 fusion.4
  29.8 0.3 fusion.6
  30.1 0.4 multiply_reduce_fusion.1
  30.5 0.2 multiply_convert_fusion.1
  30.7 0.2 fusion.37
  30.9 2.3 %collective-permute-start.4 = (f32[128,64]{1,0:T(8,128)S(1)}, f32[128,64]{1,0:T(8,128)S(1)}, u32[]{:S(2)}, u32[]{:S(2)}) collective-permute-start(f32[128,64]{1,0:T(8,128)S(1)} %slice.45), channel_id=1, source_target_pairs={{1,0},{2,1},{3,2},{4,3},{5,4},{6,5},{7,6},{8,7},{9,8},{10,9},{11,1... | collective-permute-start | bytes 98312 | tf_op jit(solution)/shard_map/ppermute | solution.py:241
  33.2 0.3 convolution_add_fusion
  33.5 1.9 %collective-permute-start.3 = (f32[128,512]{1,0:T(8,128)S(1)}, f32[128,512]{1,0:T(8,128)S(1)}, u32[]{:S(2)}, u32[]{:S(2)}) collective-permute-start(f32[128,512]{1,0:T(8,128)S(1)} %slice.43), channel_id=1, source_target_pairs={{1,0},{2,1},{3,2},{4,3},{5,4},{6,5},{7,6},{8,7},{9,8},{10,9},{11,1... | collective-permute-start | bytes 786440 | tf_op jit(solution)/shard_map/ppermute | solution.py:241
  35.4 1.5 %collective-permute-done.4 = f32[128,64]{1,0:T(8,128)S(1)} collective-permute-done((f32[128,64]{1,0:T(8,128)S(1)}, f32[128,64]{1,0:T(8,128)S(1)}, u32[]{:S(2)}, u32[]{:S(2)}) %collective-permute-start.4) | collective-permute-done | bytes 32800 | tf_op jit(solution)/shard_map/ppermute | solution.py:241
  36.9 0.3 fusion.21
  37.3 0.8 %pad_maximum_fusion.4.refs_1_ = f32[128,128]{1,0:T(8,128)} fusion(f32[128,32]{1,0:T(8,128)S(1)} %get-tuple-element.6, f32[128,32]{1,0:T(8,128)S(1)} %get-tuple-element.5), kind=kLoop, calls=%fused_computation.46 | loop fusion | flops 49152 | bytes 98304 | tf_op jit(solution)/shard_map/concatenate | solution.py:231
  38.0 31.5 %weight_gradient.1 = f32[7,64]{1,0:T(8,128)} custom-call(bf16[128,7168]{1,0:T(8,128)(2,1)} %copy-done.1, f32[128,128]{1,0:T(8,128)} %pad_maximum_fusion.4.refs_1_), custom_call_target="tpu_custom_call" | custom-call | tf_op jit(solution)/shard_map/weight_gradient/pallas_call | solution.py:221
  69.5 0.0 collective-permute-done.3
  69.5 0.7 fusion.8
  70.2 1.3 %copy.45 = f32[7,64]{1,0:T(8,128)} copy(f32[7,64]{1,0:T(8,128)} %weight_gradient.1) | data formatting | bytes 3584
  (20 shorter events, 0.1 us)
Async XLA Ops:
  0.6 24.2 %copy-start = (bf16[7168,64]{0,1:T(8,128)(2,1)S(1)}, bf16[7168,64]{0,1:T(8,128)(2,1)}, u32[]{:S(2)}) copy-start(bf16[7168,64]{0,1:T(8,128)(2,1)} %param.15) | copy-start | bytes 2752516
  1.6 20.5 %collective-permute-start.1 = (bf16[1,7168]{1,0:T(2,128)(2,1)S(1)}, bf16[1,7168]{1,0:T(2,128)(2,1)S(1)}, u32[]{:S(2)}, u32[]{:S(2)}) collective-permute-start(bf16[1,7168]{1,0:T(2,128)(2,1)S(1)} %slice_bitcast_fusion.1), channel_id=1, source_target_pairs={{1,0},{2,1},{3,2},{4,3},{5,4},{6,5},{7,6},{8,7},{9,8},{10,9},{11,1... | collective-permute-start | bytes 43016 | tf_op jit(solution)/shard_map/ppermute | solution.py:241
  17.7 11.6 %collective-permute-start = (bf16[128,512]{1,0:T(8,128)(2,1)}, bf16[128,512]{1,0:T(8,128)(2,1)S(1)}, u32[]{:S(2)}, u32[]{:S(2)}) collective-permute-start(bf16[128,512]{1,0:T(8,128)(2,1)} %bitcast.25), channel_id=1, source_target_pairs={{0,1},{1,2},{2,3},{3,4},{4,5},{5,6},{6,7},{7,8},{8,9},{9,10},{10,1... | collective-permute-start | bytes 393224 | tf_op jit(solution)/shard_map/ppermute | solution.py:241
  19.6 2.0 %copy-start.7 = (s32[1,64]{1,0:T(1,128)S(1)}, s32[1,64]{1,0:T(1,128)}, u32[]{:S(2)}) copy-start(s32[1,64]{1,0:T(1,128)} %param.9) | copy-start | bytes 772
  21.6 1.3 %copy-start.6 = (f32[7168]{0:T(1024)S(1)}, f32[7168]{0:T(1024)}, u32[]{:S(2)}) copy-start(f32[7168]{0:T(1024)} %param.14) | copy-start | bytes 86020
  23.6 1.3 %copy-start.1 = (bf16[128,7168]{1,0:T(8,128)(2,1)}, bf16[128,7168]{1,0:T(8,128)(2,1)S(1)}, u32[]{:S(2)}) copy-start(bf16[128,7168]{1,0:T(8,128)(2,1)S(1)} %multiply_convert_fusion.refs_0_) | copy-start | bytes 5505028
  24.8 3.1 %copy-start.5 = (bf16[1,128,256]{2,1,0:T(8,128)(2,1)S(1)}, bf16[1,128,256]{2,1,0:T(8,128)(2,1)}, u32[]{:S(2)}) copy-start(bf16[1,128,256]{2,1,0:T(8,128)(2,1)} %param.12) | copy-start | bytes 196612
  24.8 3.7 %copy-start.2 = (bf16[1,128,4,512]{3,2,1,0:T(4,128)(2,1)S(1)}, bf16[1,128,4,512]{3,2,1,0:T(4,128)(2,1)}, u32[]{:S(2)}) copy-start(bf16[1,128,4,512]{3,2,1,0:T(4,128)(2,1)} %param.11) | copy-start | bytes 1572868
  25.5 3.2 %copy-start.3 = (bf16[1,128,4,512]{3,2,1,0:T(4,128)(2,1)S(1)}, bf16[1,128,4,512]{3,2,1,0:T(4,128)(2,1)}, u32[]{:S(2)}) copy-start(bf16[1,128,4,512]{3,2,1,0:T(4,128)(2,1)} %param.13) | copy-start | bytes 1572868
  25.9 3.1 %collective-permute-start.2 = (bf16[128,64]{1,0:T(8,128)(2,1)S(1)}, bf16[128,64]{1,0:T(8,128)(2,1)S(1)}, u32[]{:S(2)}, u32[]{:S(2)}) collective-permute-start(bf16[128,64]{1,0:T(8,128)(2,1)S(1)} %pad_maximum_fusion.5), channel_id=1, source_target_pairs={{0,1},{1,2},{2,3},{3,4},{4,5},{5,6},{6,7},{7,8},{8,9},{9,10},{10,1... | collective-permute-start | bytes 49160 | tf_op jit(solution)/shard_map/ppermute | solution.py:241
  28.0 1.3 %copy-start.4 = (bf16[1,128,512]{2,1,0:T(8,128)(2,1)S(1)}, bf16[1,128,512]{2,1,0:T(8,128)(2,1)}, u32[]{:S(2)}) copy-start(bf16[1,128,512]{2,1,0:T(8,128)(2,1)} %param.10) | copy-start | bytes 393220
  30.9 6.0 %collective-permute-start.4 = (f32[128,64]{1,0:T(8,128)S(1)}, f32[128,64]{1,0:T(8,128)S(1)}, u32[]{:S(2)}, u32[]{:S(2)}) collective-permute-start(f32[128,64]{1,0:T(8,128)S(1)} %slice.45), channel_id=1, source_target_pairs={{1,0},{2,1},{3,2},{4,3},{5,4},{6,5},{7,6},{8,7},{9,8},{10,9},{11,1... | collective-permute-start | bytes 98312 | tf_op jit(solution)/shard_map/ppermute | solution.py:241
  33.5 36.0 %collective-permute-start.3 = (f32[128,512]{1,0:T(8,128)S(1)}, f32[128,512]{1,0:T(8,128)S(1)}, u32[]{:S(2)}, u32[]{:S(2)}) collective-permute-start(f32[128,512]{1,0:T(8,128)S(1)} %slice.43), channel_id=1, source_target_pairs={{1,0},{2,1},{3,2},{4,3},{5,4},{6,5},{7,6},{8,7},{9,8},{10,9},{11,1... | collective-permute-start | bytes 786440 | tf_op jit(solution)/shard_map/ppermute | solution.py:241

commit v2 on v1

v2 whole, which is shorter than its diff:
```python
import numpy as np
import jax
import jax.numpy as jnp
from jax import lax
from jax.experimental import pallas as pl
from jax.experimental.pallas import tpu as pltpu
from jax.sharding import PartitionSpec as P

MESH = pl.DeviceIdType.MESH
F32 = jnp.float32
BF16 = jnp.bfloat16
UNITS = (1, 3, 3)
FIRST_UNIT = (0, 1, 4)
ROW_START = (0, 256, 1024)
SENDING = (1, 2, 0)
ORDER = (4, 3, 5, 2, 6, 1, 7)


def place():
    d, c = lax.axis_index("dp"), lax.axis_index("ctx")
    return {
        "core": c % 2,
        "x": (c // 2) % 8,
        "y": (d // 8) * 2 + c // 16,
        "z": d % 8,
    }


def device(at, **moved):
    p = {**at, **moved}
    return ((p["y"] // 2) * 8 + p["z"], ((p["y"] % 2) * 8 + p["x"]) * 2 + p["core"])


STAGES = (("x", "z", "y"), ("y", "x", "z"), ("z", "x", "y"))


def step_of(axis, i):
    if axis == "x":
        return i * 14
    if axis == "z":
        return i * 224
    return (i // 2) * 1792 + (i % 2) * 112


def build_left(et_ref, left_ref):
    def body(a, carry):
        for color, (first, second, third) in enumerate(STAGES):
            units = UNITS[color]
            stride = step_of(second, 1)
            for unit in range(units):
                for q in range(2):
                    for half in range(2):
                        for pair in range(2):
                            rows = []
                            for p in (2 * pair, 2 * pair + 1):
                                base = (
                                    step_of(first, a)
                                    + step_of(third, 2 * p + half)
                                    + q * 7
                                    + FIRST_UNIT[color]
                                    + unit
                                )
                                rows.append(et_ref[pl.ds(base, 8, stride=stride), :])
                            at = ROW_START[color] + a * (units * 32) + unit * 32 + pair * 16
                            left_ref[
                                q, pl.ds(pl.multiple_of(at, 16), 16), half * 128 : half * 128 + 128
                            ] = jnp.concatenate(rows, 0).astype(BF16)
        return carry

    lax.fori_loop(0, 8, body, 0)


def rs_scratch():
    shapes = [
        pltpu.VMEM((7168, 128), F32),
        pltpu.VMEM((2, 1792, 256), BF16),
        pltpu.VMEM((1792, 128), BF16),
        pltpu.VMEM((1792, 128), BF16),
        pltpu.VMEM((1792, 128), F32),
        pltpu.SemaphoreType.DMA((3,)),
        pltpu.SemaphoreType.DMA((3,)),
        pltpu.SemaphoreType.DMA((3, 3, 8)),
        pltpu.SemaphoreType.DMA((3, 3, 8)),
    ]
    for n in UNITS:
        shapes += [
            pltpu.VMEM((8, n * 32, 128), BF16),
            pltpu.VMEM((8, n * 32, 128), BF16),
            pltpu.VMEM((n * 32, 128), F32),
            pltpu.VMEM((8, n * 4, 128), BF16),
            pltpu.VMEM((8, n * 4, 128), BF16),
            pltpu.VMEM((n * 4, 128), F32),
            pltpu.VMEM((4, n, 128), F32),
            pltpu.VMEM((8, n, 128), F32),
        ]
    return shapes


def greet(at, barrier):
    for axis in ("x", "y", "z"):
        for step in range(1, 8):
            pl.semaphore_signal(
                barrier,
                inc=1,
                device_id=device(at, **{axis: (at[axis] + step) % 8}),
                device_id_type=MESH,
            )
    pl.semaphore_signal(barrier, inc=1, device_id=device(at, core=1 - at["core"]), device_id_type=MESH)


GREETED = 22


def reduce_scatter(
    at, right, out_ref, scale, left_ref, c_send, c_recv, own, c_ss, c_rs, ss, rs, bufs, under_first, under_second
):
    core = at["core"]
    partner = device(at, core=1 - core)
    pending = []
    core_copies = {}
    for color in SENDING:
        n = UNITS[color]
        rows = pl.ds(ROW_START[color], n * 256)
        c_send[rows, :] = jnp.dot(
            left_ref[1 - core, rows, :], right, preferred_element_type=F32
        ).astype(BF16)
        copy = pltpu.make_async_remote_copy(
            src_ref=c_send.at[rows],
            dst_ref=c_recv.at[rows],
            send_sem=c_ss.at[color],
            recv_sem=c_rs.at[color],
            device_id=partner,
            device_id_type=MESH,
        )
        copy.start()
        core_copies[color] = copy
    own[...] = jnp.dot(left_ref[core], right, preferred_element_type=F32)

    def send(color, stage, source_of, target):
        axis = STAGES[color][stage]
        for step in ORDER:
            to = (at[axis] + step) % 8
            copy = pltpu.make_async_remote_copy(
                src_ref=source_of(to),
                dst_ref=target.at[step],
                send_sem=ss.at[color, stage, step],
                recv_sem=rs.at[color, stage, step],
                device_id=device(at, **{axis: to}),
                device_id_type=MESH,
            )
            copy.start()
            pending.append((color, stage, copy))

    def arrived(color, stage):
        for c, s, copy in pending:
            if (c, s) == (color, stage):
                copy.wait_recv()

    def total(first, target):
        value = first.astype(F32)
        for step in range(1, 8):
            value = value + target[step].astype(F32)
        return value

    for color in SENDING:
        n = UNITS[color]
        s1, r1, t1, s2, r2, t2, s3, r3 = bufs[color]
        core_copies[color].wait_recv()
        for a in range(8):
            rows = pl.ds(ROW_START[color] + a * n * 32, n * 32)
            s1[a] = (own[rows, :] + c_recv[rows, :].astype(F32)).astype(BF16)
        send(color, 0, lambda to: s1.at[to], r1)
    under_first()
    for color, n in enumerate(UNITS):
        s1, r1, t1, s2, r2, t2, s3, r3 = bufs[color]
        arrived(color, 0)
        t1[...] = total(s1[at[STAGES[color][0]]], r1)
        for b in range(8):
            s2[b] = t1[pl.ds(b, n * 4, stride=8), :].astype(BF16)
        send(color, 1, lambda to: s2.at[to], r2)
    under_second()
    for color, n in enumerate(UNITS):
        s1, r1, t1, s2, r2, t2, s3, r3 = bufs[color]
        arrived(color, 1)
        t2[...] = total(s2[at[STAGES[color][1]]], r2)
        for p in range(4):
            s3[p] = t2[pl.ds(p, n, stride=4), :]
        send(color, 2, lambda to: s3.at[to // 2], r3)
    for color, n in enumerate(UNITS):
        s1, r1, t1, s2, r2, t2, s3, r3 = bufs[color]
        arrived(color, 2)
        last = at[STAGES[color][2]]
        value = total(s3[last // 2], r3) * scale
        value = jnp.where(last % 2 == 0, value, pltpu.roll(value, 64, 1))
        out_ref[FIRST_UNIT[color] : FIRST_UNIT[color] + n, :] = value[:, :64]
    for copy in core_copies.values():
        copy.wait_send()
    for _, _, copy in pending:
        copy.wait_send()


score_scale = 192.0 ** (-0.5)
norm_eps = 1e-06
MERGED = 3


def rotary_tables():
    frequency = (10000.0 ** (-np.arange(32, dtype=np.float32) / 32)).astype(np.float32)
    angles = np.arange(128, dtype=np.float32)[:, None] * frequency[None, :]
    cosine = np.cos(angles.astype(np.float64)).astype(np.float32)
    sine = np.sin(angles.astype(np.float64)).astype(np.float32)
    rest = np.concatenate([np.tile(cosine, 4), -sine, sine, -sine, sine], 1)
    parts = []
    for _ in range(3):
        part = rest.astype(jnp.bfloat16)
        parts.append(part)
        rest = rest - part.astype(np.float32)
    return np.concatenate(parts, 1)


def cols(left, right):
    return lax.dot_general(left, right, (((1,), (1,)), ((), ())), preferred_element_type=F32)


def halves(value):
    low = lax.broadcasted_iota(jnp.int32, value.shape, 1) < 64
    return jnp.where(low, value, 0.0), jnp.where(low, 0.0, value)


def pack(value):
    low = lax.broadcasted_iota(jnp.int32, (64, 128), 1) < 64
    return jnp.where(low, value[:64], value[64:128])


def unpack(value):
    low = lax.broadcasted_iota(jnp.int32, (64, 128), 1) < 64
    other = pltpu.roll(value, 64, 1)
    return jnp.concatenate([jnp.where(low, value, other), jnp.where(low, other, value)], 0)


def fused_kernel(
    scale,
    lengths_hbm,
    table_hbm,
    gain_hbm,
    emb_hbm,
    w_hbm,
    lat_hbm,
    q_hbm,
    qr_hbm,
    cot_hbm,
    outlat_ref,
    outw_ref,
    lengths_ref,
    table_ref,
    gain_ref,
    emb,
    w_t,
    keys,
    q_in,
    qr,
    cot_in,
    q_all,
    cot_all,
    kr_send,
    kr_recv,
    kr1_send,
    kr1_recv,
    kg_send,
    kg_recv,
    kg1_send,
    kg1_recv,
    lg_send,
    lg_recv,
    lg_own,
    s_all,
    d_all,
    w_all,
    sg_all,
    local_sem,
    ns,
    nr,
    et,
    left,
    c_send,
    c_recv,
    own,
    c_ss,
    c_rs,
    ss,
    rs,
    *bufs,
):
    at = place()
    dp, ctx = lax.axis_index("dp"), lax.axis_index("ctx")
    after, before = (dp, (ctx + 1) % 32), (dp, (ctx + 31) % 32)
    loads = []
    pairs = (
        (lengths_hbm, lengths_ref),
        (gain_hbm, gain_ref),
        (emb_hbm, emb),
        (w_hbm, w_t),
        (table_hbm, table_ref),
        (lat_hbm, keys.at[128:256]),
        (q_hbm, q_in),
        (cot_hbm, cot_in),
        (qr_hbm, qr),
    )
    for i, (source, target) in enumerate(pairs):
        copy = pltpu.make_async_copy(source, target, local_sem.at[i])
        copy.start()
        loads.append(copy)
    barrier = pltpu.get_barrier_semaphore()
    greet(at, barrier)
    for near in (after, before):
        pl.semaphore_signal(barrier, inc=1, device_id=near, device_id_type=MESH)

    hops = []

    def hand(source, target, to):
        i = len(hops)
        copy = pltpu.make_async_remote_copy(
            src_ref=source,
            dst_ref=target,
            send_sem=ns.at[i],
            recv_sem=nr.at[i],
            device_id=to,
            device_id_type=MESH,
        )
        copy.start()
        hops.append(copy)

    offset = ctx * 128
    loads[0].wait()
    lengths = lengths_ref[...].astype(F32)
    sub64 = lax.broadcasted_iota(jnp.int32, (64, 64), 0)
    lane64 = lax.broadcasted_iota(jnp.int32, (64, 64), 1)
    ends = jnp.sum(jnp.where(lane64 <= sub64, lengths, 0.0), 1, keepdims=True)
    place_row = (offset + lax.broadcasted_iota(jnp.int32, (1, 128), 1)).astype(F32)
    start_row = jnp.max(jnp.where(ends <= place_row, ends, 0.0), 0, keepdims=True)
    shift_start = jnp.max(jnp.where(ends <= place_row - 1.0, ends, 0.0), 0, keepdims=True)
    ended = jnp.max(jnp.where(ends == place_row, 1.0, 0.0), 0, keepdims=True)
    keep_row = jnp.where((place_row >= 1.0) & (place_row < 4096.0), 1.0 - ended, 0.0)
    sub = lax.broadcasted_iota(jnp.int32, (128, 128), 0)
    lane = lax.broadcasted_iota(jnp.int32, (128, 128), 1)
    eye = sub == lane
    start_col = jnp.sum(jnp.where(eye, shift_start, 0.0), 1, keepdims=True)
    keep = jnp.sum(jnp.where(eye, keep_row, 0.0), 1, keepdims=True) > 0.5
    pos_lane = (offset - 1 + sub).astype(F32) - start_col
    chosen = jnp.where(pos_lane == lane.astype(F32), 1.0, 0.0).astype(BF16)

    loads[1].wait()
    loads[2].wait()
    loads[3].wait()

    def spans(i):
        for k in range(8):
            yield pl.ds(pl.multiple_of(i * 1024 + k * 128, 128), 128)

    def prepare(turned):
        def body(i, squares):
            for span in spans(i):
                scale_here = gain_ref[:, span]
                w_t[:, span] = (w_t[:, span].astype(F32) * scale_here).astype(BF16)
                value = emb[:, span].astype(F32)
                squares = squares + value * value
                if turned:
                    et[span, :] = (value * scale_here).T
            return squares

        return body

    def turn(i, carry):
        for span in spans(i):
            et[span, :] = (emb[:, span].astype(F32) * gain_ref[:, span]).T
        return carry

    squares = lax.fori_loop(0, MERGED, prepare(True), jnp.zeros((128, 128), F32))
    squares = lax.fori_loop(MERGED, 7, prepare(False), squares)
    raw = cols(emb[...], w_t[...])
    inverse = lax.rsqrt(jnp.sum(squares, 1, keepdims=True) / 7168.0 + norm_eps)
    loads[4].wait()
    table = jnp.dot(chosen, table_ref[...], preferred_element_type=F32)
    table = table[:, :256] + table[:, 256:512] + table[:, 512:]
    cosine, sine = table[:, :128], table[:, 128:]
    raw = raw * inverse
    raw = jnp.where(keep, jnp.concatenate([raw, raw], 1), 0.0)
    key_rope = (raw * cosine + pltpu.roll(raw, 32, 1) * sine).astype(BF16).astype(F32)
    kr_send[...] = pack(key_rope).astype(BF16)
    kr1_send[...] = key_rope[0:8]
    pl.semaphore_wait(barrier, GREETED + 2)
    hand(kr_send, kr_recv, after)
    hand(kr1_send, kr1_recv, before)
    hand(lat_hbm, keys.at[0:128], after)

    for i in (5, 6, 7, 8):
        loads[i].wait()
    q_all[...] = pltpu.einshape("thd->htd", q_in[...]).reshape(512, 512)
    cot_all[...] = pltpu.einshape("thd->htd", cot_in[...]).reshape(512, 512)
    s_all[128:256, :] = cols(keys[128:256, :], q_all[...])
    d_all[128:256, :] = cols(keys[128:256, :], cot_all[...])

    hops[2].wait_recv()
    s_all[0:128, :] = cols(keys[0:128, :], q_all[...])
    d_all[0:128, :] = cols(keys[0:128, :], cot_all[...])
    hops[0].wait_recv()
    hops[1].wait_recv()
    all_rope = jnp.concatenate([unpack(kr_recv[...].astype(F32)), key_rope], 0)
    final = lax.broadcasted_iota(jnp.int32, (256, 128), 0) == 255
    all_rope = jnp.where(final, kr1_recv[0:1, :], pltpu.roll(all_rope, 255, 0))
    ropes = [h.astype(BF16) for h in halves(all_rope)]
    key_place = (offset - 128 + lax.broadcasted_iota(jnp.int32, (256, 128), 0)).astype(F32)
    allowed = (key_place >= start_row) & (key_place <= place_row)
    parts = [jnp.zeros((256, 128), F32)] * 2
    for h in range(4):
        span = slice(h * 128, h * 128 + 128)
        query_rope = qr[:, (h // 2) * 128 : (h // 2) * 128 + 128]
        score = (s_all[:, span] + cols(ropes[h % 2], query_rope)) * score_scale
        score = jnp.where(allowed, score, -1e30)
        highest = jnp.max(score, 0, keepdims=True)
        exponent = jnp.where(allowed, jnp.exp(score - highest), 0.0)
        probs = exponent / jnp.sum(exponent, 0, keepdims=True)
        w_all[:, span] = probs.astype(BF16)
        dprobs = d_all[:, span]
        centre = jnp.sum(probs * dprobs, 0, keepdims=True)
        score_grad = (score_scale * probs * (dprobs - centre)).astype(BF16)
        sg_all[:, span] = score_grad
        parts[h % 2] = parts[h % 2] + jnp.dot(score_grad, query_rope, preferred_element_type=F32)
    wide = lax.broadcasted_iota(jnp.int32, (256, 128), 1)
    key_grad = jnp.where(wide < 64, parts[0], parts[1])
    key_grad = key_grad + pltpu.roll(key_grad, 64, 1)
    kg_send[...] = pack(key_grad[:128])
    kg1_send[...] = key_grad[248:]
    hand(kg_send, kg_recv, before)
    hand(kg1_send, kg1_recv, after)
    shifted_grad = pltpu.roll(key_grad, 1, 0)[128:]

    lax.fori_loop(MERGED, 7, turn, 0)
    build_left(et, left)

    hops[3].wait_recv()
    hops[4].wait_recv()
    handed = pltpu.roll(unpack(kg_recv[...]), 1, 0)
    shifted_grad = shifted_grad + jnp.where(sub == 0, kg1_recv[7:8, :], handed)
    raw_grad = shifted_grad * cosine - pltpu.roll(shifted_grad, 32, 1) * sine
    raw_grad = jnp.where(keep, raw_grad, 0.0) * inverse
    right = jnp.concatenate(halves(raw_grad), 0).astype(BF16)

    def latent_part():
        for half in range(2):
            span = slice(half * 128, half * 128 + 128)
            part = jnp.dot(w_all[span, :], cot_all[...], preferred_element_type=F32)
            part = part + jnp.dot(sg_all[span, :], q_all[...], preferred_element_type=F32)
            if half == 0:
                lg_send[...] = part.astype(BF16)
                hand(lg_send, lg_recv, before)
            else:
                lg_own[...] = part

    def latent_out():
        hops[5].wait_recv()
        outlat_ref[...] = (lg_own[...] + lg_recv[...].astype(F32)).astype(BF16)

    bufs = [bufs[8 * i : 8 * i + 8] for i in range(3)]
    reduce_scatter(
        at, right, outw_ref, scale, left, c_send, c_recv, own, c_ss, c_rs, ss, rs, bufs, latent_part, latent_out
    )
    for hop in hops:
        hop.wait_send()


def per_device(emb, doc_lengths, latent, q_latent, q_rope, cotangent, gain, w_rope):
    loss_scale = float(32 * 4096) ** (-0.5)
    vmem = pl.BlockSpec(memory_space=pltpu.VMEM)
    hbm = pl.BlockSpec(memory_space=pl.ANY)
    grad_latent, grad_rope_w = pl.pallas_call(
        lambda *refs: fused_kernel(loss_scale, *refs),
        out_shape=(
            pltpu.VMEM((128, 512), BF16),
            pltpu.VMEM((7, 64), F32),
        ),
        in_specs=[hbm] * 9,
        out_specs=(vmem, vmem),
        scratch_shapes=[
            pltpu.VMEM((1, 64), jnp.int32),
            pltpu.VMEM((128, 768), BF16),
            pltpu.VMEM((1, 7168), F32),
            pltpu.VMEM((128, 7168), BF16),
            pltpu.VMEM((64, 7168), BF16),
            pltpu.VMEM((256, 512), BF16),
            pltpu.VMEM((128, 4, 512), BF16),
            pltpu.VMEM((128, 256), BF16),
            pltpu.VMEM((128, 4, 512), BF16),
            pltpu.VMEM((512, 512), BF16),
            pltpu.VMEM((512, 512), BF16),
            pltpu.VMEM((64, 128), BF16),
            pltpu.VMEM((64, 128), BF16),
            pltpu.VMEM((8, 128), F32),
            pltpu.VMEM((8, 128), F32),
            pltpu.VMEM((64, 128), F32),
            pltpu.VMEM((64, 128), F32),
            pltpu.VMEM((8, 128), F32),
            pltpu.VMEM((8, 128), F32),
            pltpu.VMEM((128, 512), BF16),
            pltpu.VMEM((128, 512), BF16),
            pltpu.VMEM((128, 512), F32),
            pltpu.VMEM((256, 512), F32),
            pltpu.VMEM((256, 512), F32),
            pltpu.VMEM((256, 512), BF16),
            pltpu.VMEM((256, 512), BF16),
            pltpu.SemaphoreType.DMA((9,)),
            pltpu.SemaphoreType.DMA((6,)),
            pltpu.SemaphoreType.DMA((6,)),
        ]
        + rs_scratch(),
        compiler_params=pltpu.CompilerParams(
            collective_id=0, has_side_effects=True, vmem_limit_bytes=60 * 1024 * 1024
        ),
        name="fused",
    )(
        doc_lengths,
        jnp.asarray(rotary_tables()),
        gain[None],
        emb[0],
        w_rope.T,
        latent[0],
        q_latent[0],
        q_rope[0],
        cotangent[0],
    )
    return (grad_latent[None], grad_rope_w)


def solution(mesh):
    placed = (
        P("dp", "ctx", None),
        P("dp", None),
        P("dp", "ctx", None),
        P("dp", "ctx", None, None),
        P("dp", "ctx", None),
        P("dp", "ctx", None, None),
        P(),
        P(),
    )
    return jax.shard_map(
        per_device,
        mesh=mesh,
        in_specs=placed,
        out_specs=(P("dp", "ctx", None), P(("dp", "ctx"), None)),
        check_vma=False,
    )
```

time: 72.6 us -> 52.3 us (0.72)
  starting transfers between devices: 24 us -> 0 us
  Pallas kernels: 31.5 us -> 49.8 us
  local copies, waits for them, and re-layouts: 6.44 us -> 1.25 us
  other arithmetic: 4.45 us -> 0 us
  matrix products: 2.42 us -> 0 us
  waiting for transfers between devices: 1.64 us -> 0 us
    ppermute x5 -> x0, starting transfers between devices: 24 us -> none  [from_behind(): return lax.ppermute(block, axis, route)]
    pallas_call x1, Pallas kernels: 31.5 us -> 49.8 us  [per_device(): pl.pallas_call(lambda *refs: fused_kernel(loss_scale, *refs), out_shape=(...]
    squeeze x2 -> x0, local copies, waits for them, and re-layouts: 2.94 us -> none  [the longest x1 1.95 us: per_device(): shifted = jnp.concatenate([emb[0, 1:, :], incoming], 0)]
    dot_general x7 -> x0, matrix products: 2.42 us -> none  [the longest x3 0.96 us: contract_cols(): lax.dot_general(left, right, (((1,), (1,)), ((), ())), preferred_element_...]
    ppermute x5 -> x0, waiting for transfers between devices: 1.64 us -> none  [from_behind(): return lax.ppermute(block, axis, route)]
    unnamed x17 -> x2, local copies, waits for them, and re-layouts: 2.56 us -> 1.25 us
    reduce_sum x4 -> x0, other arithmetic: 1.03 us -> none  [the longest x1 0.68 us: normed_rows(): mean_sq = jnp.mean(values * values, axis=1, keepdims=True)]
    convert_element_type x3 -> x0, other arithmetic: 0.89 us -> none  [the longest x1 0.69 us: normed_rows(): (values * lax.rsqrt(mean_sq + norm_eps) * gain[None, :]).astype(jnp.bfloa...]
  transfers between devices with their start and end apart: 5 -> 0, of which waited for: 2 -> 0; matrix products, arithmetic and copies ran while one was open for 10% -> 0% of each run, Pallas kernels for 44% -> 0%
where the time goes in v2:
time: 52.3 us; the launch traced here: 51.7 us
  Pallas kernels  49.8 us (95%)
  local copies, waits for them, and re-layouts  1.25 us (2%)
  between operations  0.64 us (1%)
    pallas_call x1, Pallas kernels, per_device(): pl.pallas_call(lambda *refs: fused_kernel(loss_scale, *refs), out_shape=(...  49.8 us
    unnamed x2, local copies, waits for them, and re-layouts  1.25 us

profile of v2, /device:TPU:1, one launch (start us, length us, event | category | flops | bytes accessed | tf_op | source)
XLA Modules:
  0.0 51.7 jit_solution(6873004404835901061)
XLA Ops:
  0.6 49.8 %fused.1 = (bf16[128,512]{1,0:T(8,128)(2,1)S(1)}, f32[7,64]{1,0:T(8,128)S(1)}) custom-call(s32[1,64]{1,0:T(1,128)} %refs_0_.1, bf16[128,768]{1,0:T(8,128)(2,1)} %constant.2.clone.refs_1_, f32[1,7168]{1,0:T(1,128)} %bitcast.15, bf16[128,7168]{1,0:T(8,128)(2,1)} %bitcast.9, bf16[64,7168]{1,0:T(8,128)(2,1)} %bitcast.10, bf16[128,512]{1,0:T(8,128)(2,1)} %bitcast.13, ...), custom_call_target="tpu_custom_call" | custom-call | tf_op jit(solution)/shard_map/fused/pallas_call | solution.py:476
  50.5 0.7 %copy.13 = bf16[1,128,512]{2,1,0:T(8,128)(2,1)} copy(bf16[1,128,512]{2,1,0:T(8,128)(2,1)S(1)} %bitcast.8) | data formatting | bytes 262144
  51.1 0.6 %copy.14 = f32[7,64]{1,0:T(8,128)} copy(f32[7,64]{1,0:T(8,128)S(1)} %get-tuple-element.7) | data formatting | bytes 3584

commit v3 on v2

--- a/solution.py
+++ b/solution.py
@@ -9,9 +9,9 @@
 MESH = pl.DeviceIdType.MESH
 F32 = jnp.float32
 BF16 = jnp.bfloat16
-UNITS = (1, 3, 3)
-FIRST_UNIT = (0, 1, 4)
-ROW_START = (0, 256, 1024)
+UNITS = (2, 3, 2)
+FIRST_UNIT = (0, 2, 5)
+ROW_START = (0, 512, 1280)
 SENDING = (1, 2, 0)
 ORDER = (4, 3, 5, 2, 6, 1, 7)
 
@@ -31,7 +31,10 @@
     return ((p["y"] // 2) * 8 + p["z"], ((p["y"] % 2) * 8 + p["x"]) * 2 + p["core"])
 
 
-STAGES = (("x", "z", "y"), ("y", "x", "z"), ("z", "x", "y"))
+STAGES = (
+    (("x", "z", "y"), ("y", "x", "z"), ("z", "x", "y")),
+    (("x", "z", "y"), ("z", "x", "y"), ("y", "x", "z")),
+)
 
 
 def step_of(axis, i):
@@ -44,11 +47,11 @@
 
 def build_left(et_ref, left_ref):
     def body(a, carry):
-        for color, (first, second, third) in enumerate(STAGES):
-            units = UNITS[color]
-            stride = step_of(second, 1)
+        for color, units in enumerate(UNITS):
             for unit in range(units):
                 for q in range(2):
+                    first, second, third = STAGES[q][color]
+                    stride = step_of(second, 1)
                     for half in range(2):
                         for pair in range(2):
                             rows = []
@@ -97,8 +100,8 @@
 
 
 def greet(at, barrier):
-    for axis in ("x", "y", "z"):
-        for step in range(1, 8):
+    for step in ORDER:
+        for axis in ("x", "y", "z"):
             pl.semaphore_signal(
                 barrier,
                 inc=1,
@@ -112,7 +115,7 @@
 
 
 def reduce_scatter(
-    at, right, out_ref, scale, left_ref, c_send, c_recv, own, c_ss, c_rs, ss, rs, bufs, under_first, under_second
+    at, right, out_ref, scale, left_ref, c_send, c_recv, own, c_ss, c_rs, ss, rs, bufs, under_first, under_second, under_third
 ):
     core = at["core"]
     partner = device(at, core=1 - core)
@@ -134,18 +137,26 @@
         )
         copy.start()
         core_copies[color] = copy
-    own[...] = jnp.dot(left_ref[core], right, preferred_element_type=F32)
+
+    def by_core(low, high):
+        return low + core * (high - low)
+
+    def spot(color, stage):
+        return by_core(*(at[STAGES[q][color][stage]] for q in range(2)))
+
+    def peer(color, stage, to):
+        low, high = (device(at, **{STAGES[q][color][stage]: to}) for q in range(2))
+        return tuple(by_core(a, b) for a, b in zip(low, high))
 
     def send(color, stage, source_of, target):
-        axis = STAGES[color][stage]
         for step in ORDER:
-            to = (at[axis] + step) % 8
+            to = (spot(color, stage) + step) % 8
             copy = pltpu.make_async_remote_copy(
                 src_ref=source_of(to),
                 dst_ref=target.at[step],
                 send_sem=ss.at[color, stage, step],
                 recv_sem=rs.at[color, stage, step],
-                device_id=device(at, **{axis: to}),
+                device_id=peer(color, stage, to),
                 device_id_type=MESH,
             )
             copy.start()
@@ -165,6 +176,8 @@
     for color in SENDING:
         n = UNITS[color]
         s1, r1, t1, s2, r2, t2, s3, r3 = bufs[color]
+        span = pl.ds(ROW_START[color], n * 256)
+        own[span, :] = jnp.dot(left_ref[core, span, :], right, preferred_element_type=F32)
         core_copies[color].wait_recv()
         for a in range(8):
             rows = pl.ds(ROW_START[color] + a * n * 32, n * 32)
@@ -174,7 +187,7 @@
     for color, n in enumerate(UNITS):
         s1, r1, t1, s2, r2, t2, s3, r3 = bufs[color]
         arrived(color, 0)
-        t1[...] = total(s1[at[STAGES[color][0]]], r1)
+        t1[...] = total(s1[spot(color, 0)], r1)
         for b in range(8):
             s2[b] = t1[pl.ds(b, n * 4, stride=8), :].astype(BF16)
         send(color, 1, lambda to: s2.at[to], r2)
@@ -182,26 +195,31 @@
     for color, n in enumerate(UNITS):
         s1, r1, t1, s2, r2, t2, s3, r3 = bufs[color]
         arrived(color, 1)
-        t2[...] = total(s2[at[STAGES[color][1]]], r2)
+        t2[...] = total(s2[spot(color, 1)], r2)
         for p in range(4):
             s3[p] = t2[pl.ds(p, n, stride=4), :]
         send(color, 2, lambda to: s3.at[to // 2], r3)
+    for copy in core_copies.values():
+        copy.wait_send()
+    for color, stage, copy in pending:
+        if stage < 2:
+            copy.wait_send()
+    under_third()
     for color, n in enumerate(UNITS):
         s1, r1, t1, s2, r2, t2, s3, r3 = bufs[color]
         arrived(color, 2)
-        last = at[STAGES[color][2]]
+        last = spot(color, 2)
         value = total(s3[last // 2], r3) * scale
         value = jnp.where(last % 2 == 0, value, pltpu.roll(value, 64, 1))
         out_ref[FIRST_UNIT[color] : FIRST_UNIT[color] + n, :] = value[:, :64]
-    for copy in core_copies.values():
-        copy.wait_send()
-    for _, _, copy in pending:
-        copy.wait_send()
+    for color, stage, copy in pending:
+        if stage == 2:
+            copy.wait_send()
 
 
 score_scale = 192.0 ** (-0.5)
 norm_eps = 1e-06
-MERGED = 3
+MERGED = 2
 
 
 def rotary_tables():
@@ -377,6 +395,8 @@
 
     squares = lax.fori_loop(0, MERGED, prepare(True), jnp.zeros((128, 128), F32))
     squares = lax.fori_loop(MERGED, 7, prepare(False), squares)
+    pl.semaphore_wait(barrier, GREETED + 2)
+    hand(lat_hbm, keys.at[0:128], after)
     raw = cols(emb[...], w_t[...])
     inverse = lax.rsqrt(jnp.sum(squares, 1, keepdims=True) / 7168.0 + norm_eps)
     loads[4].wait()
@@ -388,23 +408,20 @@
     key_rope = (raw * cosine + pltpu.roll(raw, 32, 1) * sine).astype(BF16).astype(F32)
     kr_send[...] = pack(key_rope).astype(BF16)
     kr1_send[...] = key_rope[0:8]
-    pl.semaphore_wait(barrier, GREETED + 2)
     hand(kr_send, kr_recv, after)
     hand(kr1_send, kr1_recv, before)
-    hand(lat_hbm, keys.at[0:128], after)
 
     for i in (5, 6, 7, 8):
         loads[i].wait()
     q_all[...] = pltpu.einshape("thd->htd", q_in[...]).reshape(512, 512)
     cot_all[...] = pltpu.einshape("thd->htd", cot_in[...]).reshape(512, 512)
-    s_all[128:256, :] = cols(keys[128:256, :], q_all[...])
-    d_all[128:256, :] = cols(keys[128:256, :], cot_all[...])
-
+    lax.fori_loop(MERGED, 7, turn, 0)
+
+    hops[0].wait_recv()
+    s_all[...] = cols(keys[...], q_all[...])
+    d_all[...] = cols(keys[...], cot_all[...])
+    hops[1].wait_recv()
     hops[2].wait_recv()
-    s_all[0:128, :] = cols(keys[0:128, :], q_all[...])
-    d_all[0:128, :] = cols(keys[0:128, :], cot_all[...])
-    hops[0].wait_recv()
-    hops[1].wait_recv()
     all_rope = jnp.concatenate([unpack(kr_recv[...].astype(F32)), key_rope], 0)
     final = lax.broadcasted_iota(jnp.int32, (256, 128), 0) == 255
     all_rope = jnp.where(final, kr1_recv[0:1, :], pltpu.roll(all_rope, 255, 0))
@@ -429,18 +446,17 @@
     wide = lax.broadcasted_iota(jnp.int32, (256, 128), 1)
     key_grad = jnp.where(wide < 64, parts[0], parts[1])
     key_grad = key_grad + pltpu.roll(key_grad, 64, 1)
-    kg_send[...] = pack(key_grad[:128])
+    kg_send[...] = pack(key_grad[:128]).astype(BF16)
     kg1_send[...] = key_grad[248:]
     hand(kg_send, kg_recv, before)
     hand(kg1_send, kg1_recv, after)
     shifted_grad = pltpu.roll(key_grad, 1, 0)[128:]
 
-    lax.fori_loop(MERGED, 7, turn, 0)
     build_left(et, left)
 
     hops[3].wait_recv()
     hops[4].wait_recv()
-    handed = pltpu.roll(unpack(kg_recv[...]), 1, 0)
+    handed = pltpu.roll(unpack(kg_recv[...].astype(F32)), 1, 0)
     shifted_grad = shifted_grad + jnp.where(sub == 0, kg1_recv[7:8, :], handed)
     raw_grad = shifted_grad * cosine - pltpu.roll(shifted_grad, 32, 1) * sine
     raw_grad = jnp.where(keep, raw_grad, 0.0) * inverse
@@ -461,12 +477,14 @@
         hops[5].wait_recv()
         outlat_ref[...] = (lg_own[...] + lg_recv[...].astype(F32)).astype(BF16)
 
+    def settle():
+        for hop in hops:
+            hop.wait_send()
+
     bufs = [bufs[8 * i : 8 * i + 8] for i in range(3)]
     reduce_scatter(
-        at, right, outw_ref, scale, left, c_send, c_recv, own, c_ss, c_rs, ss, rs, bufs, latent_part, latent_out
+        at, right, outw_ref, scale, left, c_send, c_recv, own, c_ss, c_rs, ss, rs, bufs, latent_part, latent_out, settle
     )
-    for hop in hops:
-        hop.wait_send()
 
 
 def per_device(emb, doc_lengths, latent, q_latent, q_rope, cotangent, gain, w_rope):
@@ -497,8 +515,8 @@
             pltpu.VMEM((64, 128), BF16),
             pltpu.VMEM((8, 128), F32),
             pltpu.VMEM((8, 128), F32),
-            pltpu.VMEM((64, 128), F32),
-            pltpu.VMEM((64, 128), F32),
+            pltpu.VMEM((64, 128), BF16),
+            pltpu.VMEM((64, 128), BF16),
             pltpu.VMEM((8, 128), F32),
             pltpu.VMEM((8, 128), F32),
             pltpu.VMEM((128, 512), BF16),

time: 52.3 us -> 51 us (0.975)
  Pallas kernels: 49.8 us -> 48.5 us
    pallas_call x1, Pallas kernels: 49.8 us -> 48.5 us  [per_device(): pl.pallas_call(lambda *refs: fused_kernel(loss_scale, *refs), out_shape=(...]
where the time goes in v3:
time: 51 us; the launch traced here: 50.4 us
  Pallas kernels  48.5 us (95%)
  local copies, waits for them, and re-layouts  1.25 us (2%)
  between operations  0.64 us (1%)
    pallas_call x1, Pallas kernels, per_device(): pl.pallas_call(lambda *refs: fused_kernel(loss_scale, *refs), out_shape=(...  48.5 us
    unnamed x2, local copies, waits for them, and re-layouts  1.25 us

profile of v3, /device:TPU:1, one launch (start us, length us, event | category | flops | bytes accessed | tf_op | source)
XLA Modules:
  0.0 50.4 jit_solution(6919741188218975162)
XLA Ops:
  0.6 48.5 %fused.1 = (bf16[128,512]{1,0:T(8,128)(2,1)S(1)}, f32[7,64]{1,0:T(8,128)S(1)}) custom-call(s32[1,64]{1,0:T(1,128)} %refs_0_.1, bf16[128,768]{1,0:T(8,128)(2,1)} %constant.2.clone.refs_1_, f32[1,7168]{1,0:T(1,128)} %bitcast.15, bf16[128,7168]{1,0:T(8,128)(2,1)} %bitcast.9, bf16[64,7168]{1,0:T(8,128)(2,1)} %bitcast.10, bf16[128,512]{1,0:T(8,128)(2,1)} %bitcast.13, ...), custom_call_target="tpu_custom_call" | custom-call | tf_op jit(solution)/shard_map/fused/pallas_call | solution.py:494
  49.1 0.7 %copy.13 = bf16[1,128,512]{2,1,0:T(8,128)(2,1)} copy(bf16[1,128,512]{2,1,0:T(8,128)(2,1)S(1)} %bitcast.8) | data formatting | bytes 262144
  49.8 0.6 %copy.14 = f32[7,64]{1,0:T(8,128)} copy(f32[7,64]{1,0:T(8,128)S(1)} %get-tuple-element.7) | data formatting | bytes 3584

commit v4 on v3

--- a/solution.py
+++ b/solution.py
@@ -478,12 +478,13 @@
         outlat_ref[...] = (lg_own[...] + lg_recv[...].astype(F32)).astype(BF16)
 
     def settle():
+        latent_out()
         for hop in hops:
             hop.wait_send()
 
     bufs = [bufs[8 * i : 8 * i + 8] for i in range(3)]
     reduce_scatter(
-        at, right, outw_ref, scale, left, c_send, c_recv, own, c_ss, c_rs, ss, rs, bufs, latent_part, latent_out, settle
+        at, right, outw_ref, scale, left, c_send, c_recv, own, c_ss, c_rs, ss, rs, bufs, lambda: None, latent_part, settle
     )
 
 

time: 51 us -> 50.5 us (level)
  no operation moved by 1% of the time
where the time goes in v4:
time: 50.5 us; the launch traced here: 50.4 us
  Pallas kernels  48.5 us (96%)
  local copies, waits for them, and re-layouts  1.25 us (2%)
  between operations  0.64 us (1%)
    pallas_call x1, Pallas kernels, per_device(): pl.pallas_call(lambda *refs: fused_kernel(loss_scale, *refs), out_shape=(...  48.5 us
    unnamed x2, local copies, waits for them, and re-layouts  1.25 us

profile of v4, /device:TPU:1, one launch (start us, length us, event | category | flops | bytes accessed | tf_op | source)
XLA Modules:
  0.0 50.4 jit_solution(16559844820951691655)
XLA Ops:
  0.6 48.5 %fused.1 = (bf16[128,512]{1,0:T(8,128)(2,1)S(1)}, f32[7,64]{1,0:T(8,128)S(1)}) custom-call(s32[1,64]{1,0:T(1,128)} %refs_0_.1, bf16[128,768]{1,0:T(8,128)(2,1)} %constant.2.clone.refs_1_, f32[1,7168]{1,0:T(1,128)} %bitcast.15, bf16[128,7168]{1,0:T(8,128)(2,1)} %bitcast.9, bf16[64,7168]{1,0:T(8,128)(2,1)} %bitcast.10, bf16[128,512]{1,0:T(8,128)(2,1)} %bitcast.13, ...), custom_call_target="tpu_custom_call" | custom-call | tf_op jit(solution)/shard_map/fused/pallas_call | solution.py:495
  49.1 0.7 %copy.13 = bf16[1,128,512]{2,1,0:T(8,128)(2,1)} copy(bf16[1,128,512]{2,1,0:T(8,128)(2,1)S(1)} %bitcast.8) | data formatting | bytes 262144
  49.8 0.6 %copy.14 = f32[7,64]{1,0:T(8,128)} copy(f32[7,64]{1,0:T(8,128)S(1)} %get-tuple-element.7) | data formatting | bytes 3584
